TPU v7x, 32 devices: a whole 2x2x4 slice. The times are simulated.
32 devices in a mesh: blk: 8 (over z, y), line: 4 (over x, core).
Axes of the slice: x: 2, y: 2, z: 4, core: 2. Of those that a mesh axis runs over, the one named last changes fastest.
Arguments:
- density: float32 [8, 64, 4096], P('blk', 'line'), may hold values from 0.5 to 1.5
- momentum: float32 [8, 3, 64, 4096], P('blk', None, 'line'), may hold values from -0.5 to 0.5
- energy: float32 [8, 64, 4096], P('blk', 'line'), may hold values from 2 to 4
- adjoint: float32 [8, 5, 64, 4096], P('blk', None, 'line'), may hold values from -6 to 6
- partners: int32 [8, 4], P('blk'), may hold values from 0 to 7
- counts: int32 [8], P('blk'), may hold values from 1 to 4, as said below
- orient: int32 [8, 4], P('blk'), may hold values from 0 to 1
Outputs:
- residual: float32 [8, 5, 64, 4096], P('blk', None, 'line')
- correction: float32 [8], P('blk')
Inputs may be any that keep to these rules, and one draw needn't show every extreme that they name: `partners`: slots at or past counts[b] are padding and are not read. `counts`: some block lists 4 partners.
All inputs are finite; a program needn't handle non-finite values.
Results may differ from a plain program's by a relative error of at most 0.0003.
Values sent between devices are 32-bit elements; how exact they have to be, the bound alone decides.
No kernel may reach another device: no remote copies, remote signals or barrier semaphores. Data moves between devices by JAX's collectives and lax.ppermute only.
A program may use at most 64 MiB of HBM per device.

v0:
```python
import jax
import jax.numpy as jnp
from jax import lax
from jax.sharding import PartitionSpec as P

stencil_one = 0.75
stencil_two = -0.15
stencil_three = 1.0 / 60.0
gamma_less = 0.4
viscosity = 0.5
conduction = 1.5
penalty = 4.0


def difference(fields, direction, start_row, extent):
    length = fields.shape[direction]

    def shifted(offset):
        return lax.slice_in_dim(fields, 3 + offset, length - 3 + offset, axis=direction)

    shape_list = [1] * fields.ndim
    shape_list[direction] = length - 6
    global_row = (start_row + 3 + jnp.arange(length - 6, dtype=jnp.int32)).reshape(shape_list)
    central_one = shifted(1) - shifted(-1)
    central_two = shifted(2) - shifted(-2)
    central_three = shifted(3) - shifted(-3)
    interior = stencil_one * central_one + stencil_two * central_two + stencil_three * central_three
    fourth = 2.0 / 3.0 * central_one - 1.0 / 12.0 * central_two
    second = 0.5 * central_one
    forward = shifted(1) - shifted(0)
    backward = shifted(0) - shifted(-1)
    result = jnp.where((global_row == 2) | (global_row == extent - 3), fourth, interior)
    result = jnp.where((global_row == 1) | (global_row == extent - 2), second, result)
    result = jnp.where(global_row == 0, forward, result)
    result = jnp.where(global_row == extent - 1, backward, result)
    return result


def primitives(fields):
    density_raw = fields[:, 0:1]
    density_safe = jnp.where(density_raw == 0.0, 1.0, density_raw)
    velocity = fields[:, 1:4] / density_safe
    kinetic = 0.5 * jnp.sum(fields[:, 1:4] * velocity, axis=1, keepdims=True)
    pressure = gamma_less * (fields[:, 4:5] - kinetic)
    return (velocity, pressure, density_safe)


def direction_residual(fields, direction, start_row, extent, normal_index):
    velocity, pressure, density_safe = primitives(fields)
    primitive = jnp.concatenate([velocity, pressure / density_safe], axis=1)
    gradient = difference(primitive, direction, start_row, extent)
    length = fields.shape[direction]
    middle = lax.slice_in_dim(fields, 3, length - 3, axis=direction)
    mid_velocity = lax.slice_in_dim(velocity, 3, length - 3, axis=direction)
    mid_pressure = lax.slice_in_dim(pressure, 3, length - 3, axis=direction)
    normal_speed = mid_velocity[:, normal_index : normal_index + 1]
    selector = (jnp.arange(3) == normal_index).astype(fields.dtype).reshape(1, 3, 1, 1)
    convective = jnp.concatenate(
        [
            middle[:, normal_index + 1 : normal_index + 2],
            middle[:, 1:4] * normal_speed + mid_pressure * selector,
            (middle[:, 4:5] + mid_pressure) * normal_speed,
        ],
        axis=1,
    )
    viscous = jnp.concatenate(
        [
            jnp.zeros_like(normal_speed),
            viscosity * gradient[:, 0:3],
            viscosity * conduction * gradient[:, 3:4],
        ],
        axis=1,
    )
    return difference(convective - viscous, direction, start_row + 3, extent)


def per_device(density, momentum, energy, adjoint, partners, counts, orient):
    state = jnp.concatenate([density[:, None], momentum, energy[:, None]], axis=1)
    xrows = state.shape[2]
    yextent = state.shape[3]
    line_count = lax.axis_size("line")
    block_count = lax.axis_size("blk")
    xextent = xrows * line_count
    lines = lax.all_to_all(state, "line", split_axis=3, concat_axis=2, tiled=True)
    padded_lines = jnp.pad(lines, ((0, 0), (0, 0), (6, 6), (0, 0)))
    line_part = direction_residual(padded_lines, 2, -6, xextent, 0)
    xpart = lax.all_to_all(line_part, "line", split_axis=2, concat_axis=3, tiled=True)
    padded_y = jnp.pad(state, ((0, 0), (0, 0), (0, 0), (6, 6)))
    ypart = direction_residual(padded_y, 3, -6, yextent, 1)
    result = xpart + ypart
    bottom_row = state[:, :, :, 0]
    gathered = lax.all_gather(bottom_row, "blk", axis=0, tiled=True)
    slots = jnp.arange(partners.shape[1], dtype=jnp.int32)
    listed = partners[0]
    count_here = counts[0]
    weights = jnp.where(slots < count_here, 1.0 / count_here.astype(jnp.float32), jnp.float32(0.0))
    onehot = (listed[:, None] == jnp.arange(block_count, dtype=jnp.int32)[None, :]).astype(
        jnp.float32
    ) * weights[:, None]
    picked = jnp.einsum("kb,bvx->kvx", onehot, gathered, precision=lax.Precision.HIGHEST)
    signs = (
        jnp.ones((partners.shape[1], 5), jnp.float32)
        .at[:, 2]
        .set(1.0 - 2.0 * orient[0].astype(jnp.float32))
    )
    target = jnp.sum(picked * signs[:, :, None], axis=0)[None]
    result = result.at[:, :, :, yextent - 1].add(penalty * (state[:, :, :, yextent - 1] - target))
    total = lax.psum(jnp.sum(adjoint * result), "line")
    correction = (total / (xextent * yextent)).reshape(1)
    return (result, correction)


def solution(mesh):
    return jax.shard_map(
        per_device,
        mesh=mesh,
        in_specs=(
            P("blk", "line", None),
            P("blk", None, "line", None),
            P("blk", "line", None),
            P("blk", None, "line", None),
            P("blk", None),
            P("blk"),
            P("blk", None),
        ),
        out_specs=(P("blk", None, "line", None), P("blk")),
        check_vma=False,
    )
```

profile of v0, /device:TPU:0, one launch (start us, length us, event | category | flops | bytes accessed | tf_op | source)
XLA Modules:
  0.0 212.0 jit_solution(9206048323847633590)
XLA Ops:
  0.6 1.4 pad_maximum_fusion
  2.0 14.9 %copy.63 = f32[1,5,16,4096]{2,0,1,3:T(1,128)} copy(f32[1,5,16,4096]{3,2,1,0:T(8,128)S(1)} %pad_maximum_fusion) | data formatting | bytes 2621440 | tf_op jit(solution)/shard_map/concatenate | solution.py:78
  16.9 0.5 broadcast.383
  17.4 34.3 %reduce.12 = f32[4096,5,16]{2,1,0:T(8,128)} reduce(f32[4096,5,1,16]{3,2,1,0:T(1,128)} %bitcast.52, f32[]{:T(128)} %broadcast.383), dimensions={2}, to_apply=%bitcast.41.reduce_sub_computation | reduce | bytes 2621444
  51.7 9.3 %reshape.473 = f32[4,1,81920]{2,1,0:T(1,128)} reshape(f32[4096,5,16]{2,1,0:T(8,128)} %reduce.12) | data formatting | bytes 2621440
  61.0 4.2 %all-to-all-start = ((f32[4,1,81920]{2,1,0:T(1,128)}), f32[4,1,81920]{2,1,0:T(1,128)S(1)}, u32[]{:S(2)}, u32[]{:S(2)}) async-start(f32[4,1,81920]{2,1,0:T(1,128)} %reshape.473), calls=%async_computation | async-start | bytes 2621440 | tf_op jit(solution)/shard_map/all_to_all | solution.py:84
  65.3 0.6 compare_or_fusion.2
  65.9 0.6 fusion.80
  66.5 0.1 fusion.59
  66.7 0.7 compare_reduce_fusion
  67.4 0.5 multiply_reduce_fusion.2
  67.8 0.2 fusion.58
  68.1 1.3 pad_slice_fusion.35
  69.4 1.7 fusion.35
  71.2 1.0 copy-done.3
  72.2 0.7 slice-done
  72.9 0.1 copy.75
  73.0 31.8 %all-gather = f32[8,5,16,1]{2,3,1,0:T(1,128)S(1)} all-gather(f32[1,5,16,1]{2,3,1,0:T(1,128)S(1)} %copy.75), channel_id=2, replica_groups=mesh['blk'=8,'line'=4] {'blk'}, dimensions={0}, use_global_device_ids=true | all-gather | bytes 2880 | tf_op jit(solution)/shard_map/all_gather | solution.py:92
  105.4 0.6 fusion.79
  106.1 0.2 fusion.27
  106.4 0.1 copy.73
  106.5 2.2 %fusion.46 = f32[1,3,16,4102]{3,2,1,0:T(8,128)} fusion(f32[1,5,16,4096]{3,2,1,0:T(8,128)S(1)} %copy-done.1, f32[3]{0:T(128)S(1)} %compare_convert_fusion, f32[16,4102]{1,0:T(8,128)} %get-tuple-element.45, f32[16,4102]{1,0:T(8,128)} %get-tuple-element.43), kind=kLoop, calls=%fused_computation.96 | loop fusion | flops 590688 | bytes 2623372 | tf_op jit(solution)/shard_map/add | solution.py:61
  108.7 1.7 slice_multiply_fusion.3
  110.4 5.5 %reduce.13 = f32[4,81920]{1,0:T(4,128)} reduce(f32[4,1,81920]{2,1,0:T(1,128)S(1)} %all-to-all-done, f32[]{:T(128)} %broadcast.383), dimensions={1}, to_apply=%all_to_all.26.reduce_sub_computation | reduce | bytes 2621444 | tf_op jit(solution)/shard_map/all_to_all | solution.py:84
  115.9 27.3 %reshape.474 = f32[4096,5,1,16]{3,2,1,0:T(1,128)} reshape(f32[4,81920]{1,0:T(4,128)} %reduce.13) | data formatting | bytes 2621440
  143.1 19.8 %copy.64 = f32[1,5,16,4096]{3,2,1,0:T(8,128)} copy(f32[1,5,16,4096]{2,0,1,3:T(1,128)} %bitcast.53) | data formatting | bytes 2621440 | tf_op jit(solution)/shard_map/all_to_all | solution.py:84
  162.9 2.2 %all_to_all.27 = f32[1,5,16,4,1024]{4,3,2,1,0:T(4,128)S(1)} reshape(f32[1,5,16,4096]{3,2,1,0:T(8,128)} %copy.64) | data formatting | bytes 2621440 | tf_op jit(solution)/shard_map/all_to_all | solution.py:84
  165.1 0.7 copy.65
  165.9 0.2 multiply_reduce_fusion.1
  166.2 0.1 fusion.56
  166.3 0.5 copy-done.4
  166.8 1.5 fusion.20
  168.4 0.1 pad_slice_fusion.17
  168.5 0.2 fusion.43
  168.8 0.3 maximum_subtract_fusion
  169.1 1.4 fusion.12
  170.5 2.4 %copy.66 = f32[1,5,64,1024]{3,0,1,2:T(1,128)} copy(f32[1,5,64,1024]{3,2,1,0:T(8,128)S(1)} %fusion.12) | data formatting | bytes 2621440 | tf_op jit(solution)/shard_map/jit(_where)/select_n | solution.py:35
  172.9 4.3 %all-to-all-start.1 = ((f32[1,5,64,1024]{3,0,1,2:T(1,128)}), f32[1,5,64,1024]{3,0,1,2:T(1,128)}, u32[]{:S(2)}, u32[]{:S(2)}) async-start(f32[1,5,64,1024]{3,0,1,2:T(1,128)} %copy.66), calls=%async_computation.1 | async-start | bytes 2621440 | tf_op jit(solution)/shard_map/all_to_all | solution.py:87
  177.2 1.6 maximum_subtract_fusion.1
  178.7 15.7 %all-to-all-done.1 = f32[1,5,64,1024]{3,0,1,2:T(1,128)} async-done(((f32[1,5,64,1024]{3,0,1,2:T(1,128)}), f32[1,5,64,1024]{3,0,1,2:T(1,128)}, u32[]{:S(2)}, u32[]{:S(2)}) %all-to-all-start.1) | async-done | bytes 1310752 | tf_op jit(solution)/shard_map/all_to_all | solution.py:87
  194.5 1.6 copy.67
  196.1 0.1 copy.76
  196.2 2.1 fusion.6
  198.3 1.0 copy-done.2
  199.3 0.1 fusion.61
  199.4 1.8 scatter-add.4
  201.2 2.7 %multiply_reduce_fusion = f32[]{:T(128)} fusion(f32[1,5,16,4096]{3,2,1,0:T(8,128)} %param.14, f32[1,5,16,4096]{3,2,1,0:T(8,128)} %scatter-add.4), kind=kLoop, calls=%fused_computation.50 | loop fusion | flops 655359 | bytes 2621444 | tf_op jit(solution)/shard_map/reduce_sum | solution.py:108
  203.9 6.4 %psum.7 = f32[]{:T(128)} all-reduce(f32[]{:T(128)} %multiply_reduce_fusion), channel_id=1, replica_groups=mesh['blk'=8,'line'=4] {'line'}, use_global_device_ids=true, to_apply=%region_5.6 | all-reduce | flops 1 | bytes 8 | tf_op jit(solution)/shard_map/psum | solution.py:108
  (32 shorter events, 0.3 us)
Async XLA Ops:
  2.0 66.1 %copy-start = (f32[1,5,16,4096]{3,2,1,0:T(8,128)}, f32[1,5,16,4096]{3,2,1,0:T(8,128)S(1)}, u32[]{:S(2)}) copy-start(f32[1,5,16,4096]{3,2,1,0:T(8,128)S(1)} %pad_maximum_fusion) | copy-start | bytes 3932164
  61.0 49.3 %all-to-all-start = ((f32[4,1,81920]{2,1,0:T(1,128)}), f32[4,1,81920]{2,1,0:T(1,128)S(1)}, u32[]{:S(2)}, u32[]{:S(2)}) async-start(f32[4,1,81920]{2,1,0:T(1,128)} %reshape.473), calls=%async_computation | async-start | bytes 2621440 | tf_op jit(solution)/shard_map/all_to_all | solution.py:84
  71.2 1.0 copy-start.3
  72.1 0.8 slice-start
  72.1 33.3 %copy-start.7 = (s32[1,4]{1,0:T(1,128)S(1)}, s32[1,4]{1,0:T(1,128)}, u32[]{:S(2)}) copy-start(s32[1,4]{1,0:T(1,128)} %param.17) | copy-start | bytes 52
  72.1 34.0 %copy-start.8 = (s32[1,4]{1,0:T(1,128)S(1)}, s32[1,4]{1,0:T(1,128)}, u32[]{:S(2)}) copy-start(s32[1,4]{1,0:T(1,128)} %param.15) | copy-start | bytes 52
  72.1 34.3 %copy-start.1 = (f32[1,5,16,4096]{3,2,1,0:T(8,128)S(1)}, f32[1,5,16,4096]{3,2,1,0:T(8,128)}, u32[]{:S(2)}) copy-start(f32[1,5,16,4096]{3,2,1,0:T(8,128)} %copy-done) | copy-start | bytes 3932164
  166.2 0.7 copy-start.4
  166.2 0.7 copy-start.5
  166.2 0.7 copy-start.6
  172.9 21.6 %all-to-all-start.1 = ((f32[1,5,64,1024]{3,0,1,2:T(1,128)}), f32[1,5,64,1024]{3,0,1,2:T(1,128)}, u32[]{:S(2)}, u32[]{:S(2)}) async-start(f32[1,5,64,1024]{3,0,1,2:T(1,128)} %copy.66), calls=%async_computation.1 | async-start | bytes 2621440 | tf_op jit(solution)/shard_map/all_to_all | solution.py:87
  198.3 1.1 copy-start.2
where the time goes:
time: 213 us; the launch traced here: 212 us
  local copies, waits for them, and re-layouts  84.1 us (39%)
  other arithmetic  61.9 us (29%)
  blocking collectives  38.1 us (18%)
  waiting for transfers between devices  15.7 us (7%)
  starting transfers between devices  8.53 us (4%)
  between operations  3.44 us (2%)
    unnamed x22, local copies, waits for them, and re-layouts  39.8 us
    unnamed x1, other arithmetic  34.3 us
    all_gather x1, blocking collectives, per_device(): gathered = lax.all_gather(bottom_row, 'blk', axis=0, tiled=True)  31.8 us
    all_to_all x3, local copies, waits for them, and re-layouts, per_device(): lax.all_to_all(state, 'line', split_axis=3, concat_axis=2, tiled=True)  22.7 us
    all_to_all x1, waiting for transfers between devices, per_device(): lax.all_to_all(line_part, 'line', split_axis=2, concat_axis=3, tiled=True)  15.7 us
    concatenate x1, local copies, waits for them, and re-layouts, per_device(): jnp.concatenate([density[:, None], momentum, energy[:, None]], axis=1)  14.9 us
    psum x1, blocking collectives, per_device(): total = lax.psum(jnp.sum(adjoint * result), 'line')  6.37 us
    all_to_all x1, other arithmetic, per_device(): lax.all_to_all(state, 'line', split_axis=3, concat_axis=2, tiled=True)  5.48 us
  transfers between devices with their start and end apart: 2, of which 1 were waited for; matrix products, arithmetic and copies ran while one was open for 6% of the time, Pallas kernels for 0%

commit v1 on v0

--- a/solution.py
+++ b/solution.py
@@ -89,7 +89,12 @@
     ypart = direction_residual(padded_y, 3, -6, yextent, 1)
     result = xpart + ypart
     bottom_row = state[:, :, :, 0]
-    gathered = lax.all_gather(bottom_row, "blk", axis=0, tiled=True)
+    ring = [bottom_row]
+    for hop in range(7):
+        ring.append(lax.ppermute(ring[-1], "blk", [(dev, (dev + 1) % 8) for dev in range(8)]))
+    gathered = jnp.roll(
+        jnp.concatenate(ring[::-1], axis=0), (lax.axis_index("blk") + 1) * ring[0].shape[0], axis=0
+    )
     slots = jnp.arange(partners.shape[1], dtype=jnp.int32)
     listed = partners[0]
     count_here = counts[0]

time: 213 us -> 209 us (0.981)
  blocking collectives: 38.1 us -> 6.27 us
  waiting for transfers between devices: 15.7 us -> 44.1 us
  starting transfers between devices: 8.53 us -> 13.4 us
  other arithmetic: 61.9 us -> 58.6 us
  local copies, waits for them, and re-layouts: 84.1 us -> 81.7 us
    ppermute x0 -> x7, waiting for transfers between devices: none -> 35.3 us  [per_device(): lax.ppermute(ring[-1], 'blk', [(dev, (dev + 1) % 8) for dev in range(8)])]
    all_gather x1 -> x0, blocking collectives: 31.8 us -> none  [per_device(): gathered = lax.all_gather(bottom_row, 'blk', axis=0, tiled=True)]
    all_to_all x1, waiting for transfers between devices: 15.7 us -> 0.01 us  [per_device(): lax.all_to_all(line_part, 'line', split_axis=2, concat_axis=3, tiled=True)]
    all_to_all x1, waiting for transfers between devices: 0.01 us -> 8.81 us  [per_device(): lax.all_to_all(state, 'line', split_axis=3, concat_axis=2, tiled=True)]
    ppermute x0 -> x7, starting transfers between devices: none -> 4.88 us  [per_device(): lax.ppermute(ring[-1], 'blk', [(dev, (dev + 1) % 8) for dev in range(8)])]
    unnamed x22 -> x9, local copies, waits for them, and re-layouts: 39.8 us -> 38.2 us
  transfers between devices with their start and end apart: 2 -> 9, of which waited for: 1 -> 7; matrix products, arithmetic and copies ran while one was open for 6% -> 33% of each run, Pallas kernels for 0% -> 0%
where the time goes in v1:
time: 209 us; the launch traced here: 208 us
  local copies, waits for them, and re-layouts  81.7 us (39%)
  other arithmetic  58.6 us (28%)
  waiting for transfers between devices  44.1 us (21%)
  starting transfers between devices  13.4 us (6%)
  blocking collectives  6.27 us (3%)
  between operations  3.41 us (2%)
    unnamed x9, local copies, waits for them, and re-layouts  38.2 us
    ppermute x7, waiting for transfers between devices, per_device(): lax.ppermute(ring[-1], 'blk', [(dev, (dev + 1) % 8) for dev in range(8)])  35.3 us
    unnamed x1, other arithmetic  34.3 us
    all_to_all x3, local copies, waits for them, and re-layouts, per_device(): lax.all_to_all(state, 'line', split_axis=3, concat_axis=2, tiled=True)  22.7 us
    concatenate x1, local copies, waits for them, and re-layouts, per_device(): jnp.concatenate([density[:, None], momentum, energy[:, None]], axis=1)  14.7 us
    all_to_all x1, waiting for transfers between devices, per_device(): lax.all_to_all(state, 'line', split_axis=3, concat_axis=2, tiled=True)  8.81 us
    psum x1, blocking collectives, per_device(): total = lax.psum(jnp.sum(adjoint * result), 'line')  6.27 us
    all_to_all x1, other arithmetic, per_device(): lax.all_to_all(state, 'line', split_axis=3, concat_axis=2, tiled=True)  5.48 us
  transfers between devices with their start and end apart: 9, of which 7 were waited for; matrix products, arithmetic and copies ran while one was open for 33% of the time, Pallas kernels for 0%

profile of v1, /device:TPU:0, one launch (start us, length us, event | category | flops | bytes accessed | tf_op | source)
XLA Modules:
  0.0 207.8 jit_solution(11850374157598177473)
XLA Ops:
  0.6 1.4 pad_maximum_fusion
  2.0 14.7 %copy.25 = f32[1,5,16,4096]{2,0,1,3:T(1,128)} copy(f32[1,5,16,4096]{3,2,1,0:T(8,128)S(1)} %pad_maximum_fusion) | data formatting | bytes 2621440 | tf_op jit(solution)/shard_map/concatenate | solution.py:78
  16.7 0.5 broadcast.385
  17.2 34.3 %reduce.14 = f32[4096,5,16]{2,1,0:T(8,128)} reduce(f32[4096,5,1,16]{3,2,1,0:T(1,128)} %bitcast.49, f32[]{:T(128)} %broadcast.385), dimensions={2}, to_apply=%bitcast.38.reduce_sub_computation | reduce | bytes 2621444
  51.5 9.3 %reshape.473 = f32[4,1,81920]{2,1,0:T(1,128)} reshape(f32[4096,5,16]{2,1,0:T(8,128)} %reduce.14) | data formatting | bytes 2621440
  60.8 4.2 %all-to-all-start = ((f32[4,1,81920]{2,1,0:T(1,128)}), f32[4,1,81920]{2,1,0:T(1,128)S(1)}, u32[]{:S(2)}, u32[]{:S(2)}) async-start(f32[4,1,81920]{2,1,0:T(1,128)} %reshape.473), calls=%async_computation | async-start | bytes 2621440 | tf_op jit(solution)/shard_map/all_to_all | solution.py:84
  65.1 2.5 %collective-permute-start = (f32[1,5,16]{2,0,1:T(1,128)S(1)}, f32[1,5,16]{2,0,1:T(1,128)S(1)}, u32[]{:S(2)}, u32[]{:S(2)}) collective-permute-start(f32[1,5,16]{2,0,1:T(1,128)S(1)} %squeeze.9), channel_id=1, source_target_pairs={{0,4},{4,8},{8,12},{12,16},{16,20},{20,24},{24,28},{28,0},{1,5},{5... | collective-permute-start | bytes 968 | tf_op jit(solution)/shard_map/ppermute | solution.py:94
  67.7 0.1 fusion.59
  67.9 0.5 multiply_reduce_fusion.2
  68.4 0.2 fusion.58
  68.6 1.1 pad_slice_fusion.35
  69.8 1.7 fusion.35
  71.6 1.2 fusion.46
  72.8 0.7 slice_multiply_fusion.3
  73.5 8.8 %all-to-all-done = f32[4,1,81920]{2,1,0:T(1,128)S(1)} async-done(((f32[4,1,81920]{2,1,0:T(1,128)}), f32[4,1,81920]{2,1,0:T(1,128)S(1)}, u32[]{:S(2)}, u32[]{:S(2)}) %all-to-all-start) | async-done | bytes 1310752 | tf_op jit(solution)/shard_map/all_to_all | solution.py:84
  82.3 5.5 %reduce.15 = f32[4,81920]{1,0:T(4,128)} reduce(f32[4,1,81920]{2,1,0:T(1,128)S(1)} %all-to-all-done, f32[]{:T(128)} %broadcast.385), dimensions={1}, to_apply=%all_to_all.26.reduce_sub_computation | reduce | bytes 2621444 | tf_op jit(solution)/shard_map/all_to_all | solution.py:84
  87.8 27.3 %reshape.474 = f32[4096,5,1,16]{3,2,1,0:T(1,128)} reshape(f32[4,81920]{1,0:T(4,128)} %reduce.15) | data formatting | bytes 2621440
  115.1 19.8 %copy.26 = f32[1,5,16,4096]{3,2,1,0:T(8,128)} copy(f32[1,5,16,4096]{2,0,1,3:T(1,128)} %bitcast.50) | data formatting | bytes 2621440 | tf_op jit(solution)/shard_map/all_to_all | solution.py:84
  134.9 2.2 %all_to_all.27 = f32[1,5,16,4,1024]{4,3,2,1,0:T(4,128)S(1)} reshape(f32[1,5,16,4096]{3,2,1,0:T(8,128)} %copy.26) | data formatting | bytes 2621440 | tf_op jit(solution)/shard_map/all_to_all | solution.py:84
  137.0 0.7 copy.27
  137.8 0.2 multiply_reduce_fusion.1
  138.1 0.1 fusion.56
  138.2 1.5 fusion.20
  139.8 0.1 pad_slice_fusion.17
  139.9 0.2 fusion.43
  140.1 0.3 maximum_subtract_fusion
  140.5 1.4 fusion.12
  141.9 2.4 %copy.28 = f32[1,5,64,1024]{3,0,1,2:T(1,128)} copy(f32[1,5,64,1024]{3,2,1,0:T(8,128)S(1)} %fusion.12) | data formatting | bytes 2621440 | tf_op jit(solution)/shard_map/jit(_where)/select_n | solution.py:35
  144.3 4.3 %all-to-all-start.1 = ((f32[1,5,64,1024]{3,0,1,2:T(1,128)}), f32[1,5,64,1024]{3,0,1,2:T(1,128)}, u32[]{:S(2)}, u32[]{:S(2)}) async-start(f32[1,5,64,1024]{3,0,1,2:T(1,128)} %copy.28), calls=%async_computation.1 | async-start | bytes 2621440 | tf_op jit(solution)/shard_map/all_to_all | solution.py:87
  148.6 1.6 maximum_subtract_fusion.1
  150.2 0.6 compare_reduce_fusion
  150.8 0.7 fusion.78
  151.5 2.3 %collective-permute-start.1 = (f32[1,5,16]{2,0,1:T(1,128)S(1)}, f32[1,5,16]{2,0,1:T(1,128)S(1)}, u32[]{:S(2)}, u32[]{:S(2)}) collective-permute-start(f32[1,5,16]{2,0,1:T(1,128)S(1)} %collective-permute-done), channel_id=1, source_target_pairs={{0,4},{4,8},{8,12},{12,16},{16,20},{20,24},{24,28},{28,0},{1,5},{5... | collective-permute-start | bytes 968 | tf_op jit(solution)/shard_map/ppermute | solution.py:94
  154.5 3.9 %collective-permute-done.1 = f32[1,5,16]{2,0,1:T(1,128)S(1)} collective-permute-done((f32[1,5,16]{2,0,1:T(1,128)S(1)}, f32[1,5,16]{2,0,1:T(1,128)S(1)}, u32[]{:S(2)}, u32[]{:S(2)}) %collective-permute-start.1) | collective-permute-done | bytes 352 | tf_op jit(solution)/shard_map/ppermute | solution.py:94
  158.5 6.3 %collective-permute-done.2 = f32[1,5,16]{2,0,1:T(1,128)S(1)} collective-permute-done((f32[1,5,16]{2,0,1:T(1,128)S(1)}, f32[1,5,16]{2,0,1:T(1,128)S(1)}, u32[]{:S(2)}, u32[]{:S(2)}) %collective-permute-start.2) | collective-permute-done | bytes 352 | tf_op jit(solution)/shard_map/ppermute | solution.py:94
  164.7 6.3 %collective-permute-done.3 = f32[1,5,16]{2,0,1:T(1,128)S(1)} collective-permute-done((f32[1,5,16]{2,0,1:T(1,128)S(1)}, f32[1,5,16]{2,0,1:T(1,128)S(1)}, u32[]{:S(2)}, u32[]{:S(2)}) %collective-permute-start.3) | collective-permute-done | bytes 352 | tf_op jit(solution)/shard_map/ppermute | solution.py:94
  171.0 6.3 %collective-permute-done.4 = f32[1,5,16]{2,0,1:T(1,128)S(1)} collective-permute-done((f32[1,5,16]{2,0,1:T(1,128)S(1)}, f32[1,5,16]{2,0,1:T(1,128)S(1)}, u32[]{:S(2)}, u32[]{:S(2)}) %collective-permute-start.4) | collective-permute-done | bytes 352 | tf_op jit(solution)/shard_map/ppermute | solution.py:94
  177.3 6.3 %collective-permute-done.5 = f32[1,5,16]{2,0,1:T(1,128)S(1)} collective-permute-done((f32[1,5,16]{2,0,1:T(1,128)S(1)}, f32[1,5,16]{2,0,1:T(1,128)S(1)}, u32[]{:S(2)}, u32[]{:S(2)}) %collective-permute-start.5) | collective-permute-done | bytes 352 | tf_op jit(solution)/shard_map/ppermute | solution.py:94
  183.6 6.3 %collective-permute-done.6 = f32[1,5,16]{2,0,1:T(1,128)S(1)} collective-permute-done((f32[1,5,16]{2,0,1:T(1,128)S(1)}, f32[1,5,16]{2,0,1:T(1,128)S(1)}, u32[]{:S(2)}, u32[]{:S(2)}) %collective-permute-start.6) | collective-permute-done | bytes 352 | tf_op jit(solution)/shard_map/ppermute | solution.py:94
  190.0 0.2 fusion.27
  190.2 0.1 copy.31
  190.4 1.6 copy.29
  191.9 0.1 copy.32
  192.0 2.1 %fusion.6 = f32[1,5,16,4096]{3,2,1,0:T(8,128)S(1)} fusion(f32[1,5,16,4096]{3,2,1,0:T(8,128)S(1)} %bitcast.53, f32[1,5,16,4102]{3,2,1,0:T(8,128)S(1)} %maximum_subtract_fusion.1, pred[4096]{0:T(1024)(128)(4,1)S(1)} %get-tuple-element.59, pred[4096]{0:T(1024)(128)(4,1)S(1)} %get-tuple-element.58, pred[4096]{0:T(1024)(128)(4,1)S(1)} %get-tuple-element.56, ...), kind=kLoop, calls=%fused_computation.39 | loop fusion | flops 6225920 | bytes 11812864 | tf_op jit(solution)/shard_map/add | solution.py:90
  194.2 1.0 copy-done
  195.3 1.8 scatter-add.4
  197.1 2.7 %multiply_reduce_fusion = f32[]{:T(128)} fusion(f32[1,5,16,4096]{3,2,1,0:T(8,128)} %param.14, f32[1,5,16,4096]{3,2,1,0:T(8,128)} %scatter-add.4), kind=kLoop, calls=%fused_computation.50 | loop fusion | flops 655359 | bytes 2621444 | tf_op jit(solution)/shard_map/reduce_sum | solution.py:113
  199.7 6.3 %psum.7 = f32[]{:T(128)} all-reduce(f32[]{:T(128)} %multiply_reduce_fusion), channel_id=1, replica_groups=mesh['blk'=8,'line'=4] {'line'}, use_global_device_ids=true, to_apply=%region_5.6 | all-reduce | flops 1 | bytes 8 | tf_op jit(solution)/shard_map/psum | solution.py:113
  (33 shorter events, 0.6 us)
Async XLA Ops:
  60.8 21.5 %all-to-all-start = ((f32[4,1,81920]{2,1,0:T(1,128)}), f32[4,1,81920]{2,1,0:T(1,128)S(1)}, u32[]{:S(2)}, u32[]{:S(2)}) async-start(f32[4,1,81920]{2,1,0:T(1,128)} %reshape.473), calls=%async_computation | async-start | bytes 2621440 | tf_op jit(solution)/shard_map/all_to_all | solution.py:84
  65.1 86.4 %collective-permute-start = (f32[1,5,16]{2,0,1:T(1,128)S(1)}, f32[1,5,16]{2,0,1:T(1,128)S(1)}, u32[]{:S(2)}, u32[]{:S(2)}) collective-permute-start(f32[1,5,16]{2,0,1:T(1,128)S(1)} %squeeze.9), channel_id=1, source_target_pairs={{0,4},{4,8},{8,12},{12,16},{16,20},{20,24},{24,28},{28,0},{1,5},{5... | collective-permute-start | bytes 968 | tf_op jit(solution)/shard_map/ppermute | solution.py:94
  144.3 46.1 %all-to-all-start.1 = ((f32[1,5,64,1024]{3,0,1,2:T(1,128)}), f32[1,5,64,1024]{3,0,1,2:T(1,128)}, u32[]{:S(2)}, u32[]{:S(2)}) async-start(f32[1,5,64,1024]{3,0,1,2:T(1,128)} %copy.28), calls=%async_computation.1 | async-start | bytes 2621440 | tf_op jit(solution)/shard_map/all_to_all | solution.py:87
  148.6 2.3 %copy-start.1 = (s32[1,4]{1,0:T(1,128)S(1)}, s32[1,4]{1,0:T(1,128)}, u32[]{:S(2)}) copy-start(s32[1,4]{1,0:T(1,128)} %param.17) | copy-start | bytes 52
  148.6 41.4 %copy-start.2 = (s32[1,4]{1,0:T(1,128)S(1)}, s32[1,4]{1,0:T(1,128)}, u32[]{:S(2)}) copy-start(s32[1,4]{1,0:T(1,128)} %param.15) | copy-start | bytes 52
  151.5 6.9 %collective-permute-start.1 = (f32[1,5,16]{2,0,1:T(1,128)S(1)}, f32[1,5,16]{2,0,1:T(1,128)S(1)}, u32[]{:S(2)}, u32[]{:S(2)}) collective-permute-start(f32[1,5,16]{2,0,1:T(1,128)S(1)} %collective-permute-done), channel_id=1, source_target_pairs={{0,4},{4,8},{8,12},{12,16},{16,20},{20,24},{24,28},{28,0},{1,5},{5... | collective-permute-start | bytes 968 | tf_op jit(solution)/shard_map/ppermute | solution.py:94
  158.5 6.3 %collective-permute-start.2 = (f32[1,5,16]{2,0,1:T(1,128)S(1)}, f32[1,5,16]{2,0,1:T(1,128)S(1)}, u32[]{:S(2)}, u32[]{:S(2)}) collective-permute-start(f32[1,5,16]{2,0,1:T(1,128)S(1)} %collective-permute-done.1), channel_id=1, source_target_pairs={{0,4},{4,8},{8,12},{12,16},{16,20},{20,24},{24,28},{28,0},{1,5},{5... | collective-permute-start | bytes 968 | tf_op jit(solution)/shard_map/ppermute | solution.py:94
  164.7 6.3 %collective-permute-start.3 = (f32[1,5,16]{2,0,1:T(1,128)S(1)}, f32[1,5,16]{2,0,1:T(1,128)S(1)}, u32[]{:S(2)}, u32[]{:S(2)}) collective-permute-start(f32[1,5,16]{2,0,1:T(1,128)S(1)} %collective-permute-done.2), channel_id=1, source_target_pairs={{0,4},{4,8},{8,12},{12,16},{16,20},{20,24},{24,28},{28,0},{1,5},{5... | collective-permute-start | bytes 968 | tf_op jit(solution)/shard_map/ppermute | solution.py:94
  171.0 6.3 %collective-permute-start.4 = (f32[1,5,16]{2,0,1:T(1,128)S(1)}, f32[1,5,16]{2,0,1:T(1,128)S(1)}, u32[]{:S(2)}, u32[]{:S(2)}) collective-permute-start(f32[1,5,16]{2,0,1:T(1,128)S(1)} %collective-permute-done.3), channel_id=1, source_target_pairs={{0,4},{4,8},{8,12},{12,16},{16,20},{20,24},{24,28},{28,0},{1,5},{5... | collective-permute-start | bytes 968 | tf_op jit(solution)/shard_map/ppermute | solution.py:94
  177.3 6.3 %collective-permute-start.5 = (f32[1,5,16]{2,0,1:T(1,128)S(1)}, f32[1,5,16]{2,0,1:T(1,128)S(1)}, u32[]{:S(2)}, u32[]{:S(2)}) collective-permute-start(f32[1,5,16]{2,0,1:T(1,128)S(1)} %collective-permute-done.4), channel_id=1, source_target_pairs={{0,4},{4,8},{8,12},{12,16},{16,20},{20,24},{24,28},{28,0},{1,5},{5... | collective-permute-start | bytes 968 | tf_op jit(solution)/shard_map/ppermute | solution.py:94
  183.6 6.3 %collective-permute-start.6 = (f32[1,5,16]{2,0,1:T(1,128)S(1)}, f32[1,5,16]{2,0,1:T(1,128)S(1)}, u32[]{:S(2)}, u32[]{:S(2)}) collective-permute-start(f32[1,5,16]{2,0,1:T(1,128)S(1)} %collective-permute-done.5), channel_id=1, source_target_pairs={{0,4},{4,8},{8,12},{12,16},{16,20},{20,24},{24,28},{28,0},{1,5},{5... | collective-permute-start | bytes 968 | tf_op jit(solution)/shard_map/ppermute | solution.py:94
  194.1 1.1 copy-start
